TPU v7x, 512 devices: a whole 4x8x8 slice. The times are simulated.
512 devices in a mesh: row: 16 (over y, core), col: 32 (over z, x).
Axes of the slice: x: 4, y: 8, z: 8, core: 2. Of those that a mesh axis runs over, the one named last changes fastest.
Arguments:
- query_matrix: bfloat16 [128, 512, 768], P('row', 'col'), may hold values from -6 to 16.133757
- key_matrix: bfloat16 [128, 512, 768], P('row', 'col'), may hold values from -6 to 6
- value_matrix: bfloat16 [128, 512, 768], P('row', 'col'), may hold values from -6 to 6
- tissue: int32 [128, 512], replicated, may hold values 0 or 1
- dilation_levels: int32 [16], replicated, may hold values from 0 to 2
- segment_levels: int32 [16], replicated, may hold values from 0 to 2
- output_matrix: bfloat16 [768, 768], replicated, may hold values from -0.21875 to 0.21875
Outputs:
- encoded: bfloat16 [128, 512, 768], P('row', 'col')
Inputs may be any that keep to these rules, and one draw needn't show every extreme that they name: 1 marks a tissue tile, 0 background. Head h uses the dilation 8 * 2^dilation_levels[h]. Head h uses segments of 512 / 2^segment_levels[h] tiles of a grid row.
All inputs are finite; a program needn't handle non-finite values.
Results may differ from a plain program's by a relative error of at most 0.0055.
Values may be sent and summed in bfloat16 or wider, within the bound.
No kernel may reach another device: no remote copies, remote signals or barrier semaphores. Data moves between devices by JAX's collectives and lax.ppermute only.
A program may use at most 64 MiB of HBM per device.

v0:
```python
import math
import jax
import jax.numpy as jnp
import numpy as np
from jax import lax
from jax.sharding import PartitionSpec as P

HEAD_COUNT = 16
R = 8
DILATION_MIN = 8
NEG_FILL = -1e30


def padded_2(x, sides, width):
    for axis, dim in sides:
        peers, length = (lax.axis_size(axis), x.shape[dim])
        up = [(i, (i + 1) % peers) for i in range(peers - 1)]
        down = [(j, i) for i, j in up]
        last = lax.slice_in_dim(x, length - width, length, axis=dim)
        first = lax.slice_in_dim(x, 0, width, axis=dim)
        before = lax.ppermute(last, axis, up)
        after = lax.ppermute(first, axis, down)
        x = jnp.concatenate([before, x, after], axis=dim)
    return x


def window_static(device_rows, device_columns):
    region_rows = np.arange(device_rows + 2 * R) - R
    query_rows = np.arange(device_rows)
    region_cols = np.arange(device_columns + 2 * R) - R
    query_cols = np.arange(device_columns)
    near_rows = np.abs(region_rows[None, :] - query_rows[:, None]) <= R
    near_cols = np.abs(region_cols[None, :] - query_cols[:, None]) <= R
    same_rows = region_rows[None, :] == query_rows[:, None]
    same_cols = region_cols[None, :] == query_cols[:, None]
    near_both = near_rows[:, None, :, None] & near_cols[None, :, None, :]
    self_both = same_rows[:, None, :, None] & same_cols[None, :, None, :]
    return (near_both, self_both)


def window_part(queries, key_region, value_region, permitted_mask, group_size):
    head_dimension = queries.shape[-1] // HEAD_COUNT
    scale = 1.0 / math.sqrt(head_dimension)
    numerators, maxima, totals = ([], [], [])
    for head_first in range(0, HEAD_COUNT, group_size):
        lower = head_first * head_dimension
        upper = (head_first + group_size) * head_dimension
        query_grp = queries[:, lower:upper].reshape(queries.shape[0], group_size, head_dimension)
        key_grp = key_region[:, lower:upper].reshape(
            key_region.shape[0], group_size, head_dimension
        )
        value_grp = value_region[:, lower:upper].reshape(
            value_region.shape[0], group_size, head_dimension
        )
        scores = (
            jnp.einsum("qhd,khd->hqk", query_grp, key_grp, preferred_element_type=jnp.float32)
            * scale
        )
        scores = jnp.where(permitted_mask[None], scores, NEG_FILL)
        highest = jnp.max(scores, axis=-1)
        exp_terms = jnp.exp(scores - highest[..., None])
        totals.append(jnp.sum(exp_terms, axis=-1))
        numerators.append(
            jnp.einsum(
                "hqk,khd->qhd",
                exp_terms.astype(jnp.bfloat16),
                value_grp,
                preferred_element_type=jnp.float32,
            )
        )
        maxima.append(highest)
    return (
        jnp.concatenate(numerators, axis=1),
        jnp.concatenate(maxima, axis=0).T,
        jnp.concatenate(totals, axis=0).T,
    )


def dilation_valid_mask(
    tissue,
    row_indices,
    head_indices,
    column_indices,
    dilation_levels,
    segment_levels,
    selected_count,
    column_total,
):
    key_columns = (
        jnp.arange(selected_count, dtype=jnp.int32)[None, :] * DILATION_MIN
        + (head_indices % DILATION_MIN)[:, None]
    )
    tissue_keys = tissue[row_indices[:, None], key_columns]
    dilation_stride = jnp.left_shift(jnp.int32(DILATION_MIN), dilation_levels[head_indices])
    segment = jnp.right_shift(jnp.int32(column_total), segment_levels[head_indices])
    phase_ok = key_columns % dilation_stride[:, None] == (head_indices % dilation_stride)[:, None]
    key_seg = key_columns // segment[:, None]
    query_seg = column_indices[None, :] // segment[:, None]
    same_seg = key_seg[:, None, :] == query_seg[:, :, None]
    return same_seg & ((tissue_keys == 1) & phase_ok)[:, None, :]


def dilation_in_grid(queries, keys_sel, values_sel, permitted_mask):
    scale = 1.0 / math.sqrt(queries.shape[-1])
    scores = (
        jnp.einsum("rchw,rshw->rhcs", queries, keys_sel, preferred_element_type=jnp.float32) * scale
    )
    scores = jnp.where(permitted_mask, scores, NEG_FILL)
    highest = jnp.max(scores, axis=-1)
    exp_terms = jnp.where(permitted_mask, jnp.exp(scores - highest[..., None]), 0.0)
    totals = jnp.sum(exp_terms, axis=-1)
    softmax_numer = jnp.einsum(
        "rhcs,rshw->rchw",
        exp_terms.astype(jnp.bfloat16),
        values_sel,
        preferred_element_type=jnp.float32,
    )
    return (softmax_numer, highest, totals)


def merge_partials(
    neighbour_numer, neighbour_max, neighbour_sum, dilation_numer, dilation_score_max, dilation_sum
):
    running_maximum = jnp.maximum(neighbour_max, dilation_score_max)
    neighbour_rescale = jnp.exp(neighbour_max - running_maximum)
    dilation_rescale = jnp.exp(dilation_score_max - running_maximum)
    softmax_numer = (
        neighbour_rescale[..., None] * neighbour_numer
        + dilation_rescale[..., None] * dilation_numer
    )
    softmax_denom = neighbour_rescale * neighbour_sum + dilation_rescale * dilation_sum
    return softmax_numer / softmax_denom[..., None]


def per_device(
    query_matrix, key_matrix, value_matrix, tissue, dilation_levels, segment_levels, output_matrix
):
    device_rows, device_columns, model_width = query_matrix.shape
    head_dimension = model_width // HEAD_COUNT
    col_count = lax.axis_size("col")
    column_total = device_columns * col_count
    selected_count = column_total // DILATION_MIN
    local_selection = device_columns // DILATION_MIN
    row_offset = lax.axis_index("row") * device_rows
    column_offset = lax.axis_index("col") * device_columns
    packed = jnp.concatenate([key_matrix, value_matrix], axis=-1)
    padded = padded_2(packed, (("row", 0), ("col", 1)), R)
    key_region = padded[:, :, :model_width].reshape(-1, model_width)
    value_region = padded[:, :, model_width:].reshape(-1, model_width)
    tissue_pad = jnp.pad(tissue, R)
    tissue_reg = lax.dynamic_slice(
        tissue_pad, (row_offset, column_offset), (device_rows + 2 * R, device_columns + 2 * R)
    )
    near_both, self_both = window_static(device_rows, device_columns)
    permitted_mask = jnp.asarray(near_both) & (tissue_reg[None, None] == 1) | jnp.asarray(self_both)
    permitted_mask = permitted_mask.reshape(device_rows * device_columns, -1)
    neighbour_numer, neighbour_max, neighbour_sum = window_part(
        query_matrix.reshape(-1, model_width), key_region, value_region, permitted_mask, 2
    )
    phase_table = np.arange(HEAD_COUNT)[None, :] % DILATION_MIN == np.arange(DILATION_MIN)[:, None]
    phase_table = jnp.asarray(phase_table)[None, None, :, :, None]
    key_phases = key_matrix.reshape(
        device_rows, local_selection, DILATION_MIN, HEAD_COUNT, head_dimension
    )
    value_phases = value_matrix.reshape(
        device_rows, local_selection, DILATION_MIN, HEAD_COUNT, head_dimension
    )
    zero_entry = jnp.zeros((), jnp.bfloat16)
    key_selected = jnp.sum(
        jnp.where(phase_table, key_phases, zero_entry), axis=2, dtype=jnp.bfloat16
    ).reshape(device_rows, local_selection, model_width)
    value_selected = jnp.sum(
        jnp.where(phase_table, value_phases, zero_entry), axis=2, dtype=jnp.bfloat16
    ).reshape(device_rows, local_selection, model_width)
    token_count = device_rows * HEAD_COUNT
    k_all, v_all = (
        lax.all_gather(key_selected, "col", axis=1, tiled=True),
        lax.all_gather(value_selected, "col", axis=1, tiled=True),
    )
    key_grid = k_all.reshape(device_rows, selected_count, HEAD_COUNT, head_dimension)
    value_grid = v_all.reshape(device_rows, selected_count, HEAD_COUNT, head_dimension)
    item_ids = jnp.arange(token_count, dtype=jnp.int32)
    column_indices = column_offset + jnp.arange(device_columns, dtype=jnp.int32)
    dilation_permitted = dilation_valid_mask(
        tissue,
        row_offset + item_ids // HEAD_COUNT,
        item_ids % HEAD_COUNT,
        column_indices,
        dilation_levels,
        segment_levels,
        selected_count,
        column_total,
    )
    dilation_permitted = dilation_permitted.reshape(
        device_rows, HEAD_COUNT, device_columns, selected_count
    )
    query_grid = query_matrix.reshape(device_rows, device_columns, HEAD_COUNT, head_dimension)
    grid_numer, grid_max, grid_sum = dilation_in_grid(
        query_grid, key_grid, value_grid, dilation_permitted
    )
    dilation_numer = grid_numer.reshape(-1, HEAD_COUNT, head_dimension)
    dilation_score_max = grid_max.transpose(0, 2, 1).reshape(-1, HEAD_COUNT)
    dilation_sum = grid_sum.transpose(0, 2, 1).reshape(-1, HEAD_COUNT)
    attended = (
        merge_partials(
            neighbour_numer,
            neighbour_max,
            neighbour_sum,
            dilation_numer,
            dilation_score_max,
            dilation_sum,
        )
        .reshape(-1, model_width)
        .astype(jnp.bfloat16)
    )
    encoded = jnp.dot(attended, output_matrix, preferred_element_type=jnp.float32).astype(
        jnp.bfloat16
    )
    return encoded.reshape(device_rows, device_columns, model_width)


def solution(mesh):
    in_specs = (
        P("row", "col", None),
        P("row", "col", None),
        P("row", "col", None),
        P(),
        P(),
        P(),
        P(),
    )
    out_specs = P("row", "col", None)
    return jax.shard_map(
        per_device, mesh=mesh, in_specs=in_specs, out_specs=out_specs, check_vma=False
    )
```

profile of v0, /device:TPU:56, one launch (start us, length us, event | category | flops | bytes accessed | tf_op | source)
XLA Modules:
  0.0 276.5 jit_solution(2129543870219069759)
XLA Ops:
  2.0 2.7 collective-permute-start.1
  4.7 2.4 collective-permute-start
  7.2 1.9 fusion.111
  9.1 10.0 %fusion.98 = s32[128]{0:T(128)S(1)} fusion(s32[]{:T(128)} %bitcast.62, s32[]{:T(128)} %bitcast.63, s32[]{:T(128)} %bitcast.64, s32[]{:T(128)} %bitcast.65, s32[]{:T(128)} %bitcast.66, s32[]{:T(128)} %bitcast.68, s32[]{:T(128)} %bitcast.67, s32[]{:T(128)} %bitcast.53, s32[]{:T(128)} %bitcast.54, s32[]{:T(128)} %bitcast.55, s32[]{:T(128)} %bitcast.56, ...), kind=kLoop, calls=%fused_computation.190 | loop fusion | flops 5120 | bytes 576 | tf_op jit(solution)/shard_map/shift_left | solution.py:94
  19.3 1.6 reshape.570
  20.9 1.6 reshape.584
  23.2 10.0 %fusion.97 = s32[128]{0:T(128)S(1)} fusion(s32[]{:T(128)} %bitcast.45, s32[]{:T(128)} %bitcast.46, s32[]{:T(128)} %bitcast.47, s32[]{:T(128)} %bitcast.48, s32[]{:T(128)} %bitcast.49, s32[]{:T(128)} %bitcast.51, s32[]{:T(128)} %bitcast.50, s32[]{:T(128)} %bitcast.28, s32[]{:T(128)} %bitcast.30, s32[]{:T(128)} %bitcast.32, s32[]{:T(128)} %bitcast.34, ...), kind=kLoop, calls=%fused_computation.189 | loop fusion | flops 5120 | bytes 576 | tf_op jit(solution)/shard_map/shift_right_arithmetic | solution.py:95
  33.5 65.0 %gather_fusion = s32[8192]{0:T(1024)S(1)} fusion(s32[128,512]{1,0:T(8,128)S(1)} %copy-done.1, s32[8192]{0:T(1024)S(1)} %reshape.613), kind=kCustom, calls=%fused_computation | custom fusion | bytes 131072 | tf_op jit(solution)/shard_map/gather | solution.py:93
  101.4 1.4 add_select_fusion
  102.8 2.2 and_or_fusion
  105.7 55.9 %all_gather.6 = bf16[8,64,768]{2,0,1:T(8,128)(2,1)S(1)} all-gather(bf16[8,2,768]{2,0,1:T(8,128)(2,1)S(1)} %copy.179), channel_id=1, replica_groups=mesh['row'=16,'col'=32] {'col'}, dimensions={1}, use_global_device_ids=true | all-gather | bytes 811008 | tf_op jit(solution)/shard_map/all_gather | solution.py:177
  162.2 1.6 copy.180
  163.9 2.0 fusion.113
  165.9 1.3 pad_maximum_fusion.1
  168.4 3.9 %collective-permute-start.2 = (bf16[24,8,1536]{2,1,0:T(8,128)(2,1)}, bf16[24,8,1536]{2,1,0:T(8,128)(2,1)}, u32[]{:S(2)}, u32[]{:S(2)}) collective-permute-start(bf16[24,8,1536]{2,1,0:T(8,128)(2,1)} %get-tuple-element.28), channel_id=1, source_target_pairs={{0,1},{1,2},{2,3},{3,4},{4,5},{5,6},{6,7},{7,8},{8,9},{9,10},{10,1... | collective-permute-start | bytes 1769480 | tf_op jit(solution)/shard_map/ppermute | solution.py:21
  172.2 1.3 collective-permute-start.3
  174.6 1.5 copy.227
  176.0 1.4 copy.225
  183.5 51.7 %all_gather.7 = bf16[8,64,768]{2,0,1:T(8,128)(2,1)S(1)} all-gather(bf16[8,2,768]{2,0,1:T(8,128)(2,1)S(1)} %copy.199), channel_id=1, replica_groups=mesh['row'=16,'col'=32] {'col'}, dimensions={1}, use_global_device_ids=true | all-gather | bytes 811008 | tf_op jit(solution)/shard_map/all_gather | solution.py:178
  235.2 1.6 copy.200
  236.8 2.4 convolution_bitcast_fusion
  240.9 1.7 pad_maximum_fusion
  242.8 1.2 fusion.108
  244.0 1.7 copy.235
  245.7 1.7 copy.234
  247.4 1.7 copy.233
  253.2 1.2 fusion.107
  254.4 1.7 copy.226
  259.7 1.2 fusion.25
  268.1 1.4 concatenate.24
  270.4 1.6 fusion.19
  272.9 1.4 concatenate.27
  (164 shorter events, 35.9 us)
Async XLA Ops:
  0.0 275.4 %copy-start = (bf16[768,768]{1,0:T(8,128)(2,1)S(1)}, bf16[768,768]{1,0:T(8,128)(2,1)}, u32[]{:S(2)}) copy-start(bf16[768,768]{1,0:T(8,128)(2,1)} %param.16) | copy-start | bytes 3538948
  0.0 22.5 %copy-start.23 = (s32[16]{0:T(128)S(1)}, s32[16]{0:T(128)}, u32[]{:S(2)}) copy-start(s32[16]{0:T(128)} %param.15) | copy-start | bytes 196
  0.0 33.5 %copy-start.1 = (s32[128,512]{1,0:T(8,128)S(1)}, s32[128,512]{1,0:T(8,128)}, u32[]{:S(2)}) copy-start(s32[128,512]{1,0:T(8,128)} %param.13) | copy-start | bytes 786436
  2.0 163.9 %collective-permute-start.1 = (bf16[8,16,1536]{2,1,0:T(8,128)(2,1)S(1)}, bf16[8,16,1536]{2,1,0:T(8,128)(2,1)}, u32[]{:S(2)}, u32[]{:S(2)}) collective-permute-start(bf16[8,16,1536]{2,1,0:T(8,128)(2,1)S(1)} %constant_dynamic-update-slice_fusion), channel_id=1, source_target_pairs={{32,0},{64,32},{96,64},{128,96},{160,128},{192,160},{224,192},{256... | collective-permute-start | bytes 1179656 | tf_op jit(solution)/shard_map/ppermute | solution.py:22
  4.7 161.2 %collective-permute-start = (bf16[8,16,1536]{2,1,0:T(8,128)(2,1)S(1)}, bf16[8,16,1536]{2,1,0:T(8,128)(2,1)}, u32[]{:S(2)}, u32[]{:S(2)}) collective-permute-start(bf16[8,16,1536]{2,1,0:T(8,128)(2,1)S(1)} %constant_dynamic-update-slice_fusion), channel_id=1, source_target_pairs={{0,32},{32,64},{64,96},{96,128},{128,160},{160,192},{192,224},{224... | collective-permute-start | bytes 1179656 | tf_op jit(solution)/shard_map/ppermute | solution.py:21
  33.5 65.1 %copy-start.4 = (bf16[8,16,768]{2,1,0:T(8,128)(2,1)S(1)}, bf16[8,16,768]{2,1,0:T(8,128)(2,1)}, u32[]{:S(2)}) copy-start(bf16[8,16,768]{2,1,0:T(8,128)(2,1)} %param.10) | copy-start | bytes 589828
  33.5 65.9 %copy-start.40 = (pred[8,16]{1,0:T(8,128)(4,1)S(1)}, pred[8,16]{1,0:T(8,128)(4,1)}, u32[]{:S(2)}) copy-start(pred[8,16]{1,0:T(8,128)(4,1)} %constant.110.clone) | copy-start | bytes 388
  101.4 73.2 %copy-start.5 = (s32[8,16,64]{2,1,0:T(8,128)}, s32[8,16,64]{2,1,0:T(8,128)S(1)}, u32[]{:S(2)}) copy-start(s32[8,16,64]{2,1,0:T(8,128)S(1)} %add_select_fusion.1) | copy-start | bytes 98308
  165.9 16.7 %copy-start.7 = (f32[8,16,16]{2,1,0:T(8,128)}, f32[8,16,16]{2,1,0:T(8,128)S(1)}, u32[]{:S(2)}) copy-start(f32[8,16,16]{2,1,0:T(8,128)S(1)} %get-tuple-element.72) | copy-start | bytes 24580
  167.2 10.3 %copy-start.22 = (bf16[128,96]{1,0:T(8,128)(2,1)S(1)}, bf16[128,96]{1,0:T(8,128)(2,1)}, u32[]{:S(2)}) copy-start(bf16[128,96]{1,0:T(8,128)(2,1)} %get-tuple-element.32) | copy-start | bytes 73732
  167.2 11.0 %copy-start.21 = (bf16[128,96]{1,0:T(8,128)(2,1)S(1)}, bf16[128,96]{1,0:T(8,128)(2,1)}, u32[]{:S(2)}) copy-start(bf16[128,96]{1,0:T(8,128)(2,1)} %get-tuple-element.33) | copy-start | bytes 73732
  167.2 11.7 %copy-start.20 = (bf16[128,96]{1,0:T(8,128)(2,1)S(1)}, bf16[128,96]{1,0:T(8,128)(2,1)}, u32[]{:S(2)}) copy-start(bf16[128,96]{1,0:T(8,128)(2,1)} %get-tuple-element.34) | copy-start | bytes 73732
  167.2 12.4 %copy-start.19 = (bf16[128,96]{1,0:T(8,128)(2,1)S(1)}, bf16[128,96]{1,0:T(8,128)(2,1)}, u32[]{:S(2)}) copy-start(bf16[128,96]{1,0:T(8,128)(2,1)} %get-tuple-element.35) | copy-start | bytes 73732
  167.2 13.1 %copy-start.18 = (bf16[128,96]{1,0:T(8,128)(2,1)S(1)}, bf16[128,96]{1,0:T(8,128)(2,1)}, u32[]{:S(2)}) copy-start(bf16[128,96]{1,0:T(8,128)(2,1)} %get-tuple-element.36) | copy-start | bytes 73732
  167.3 14.4 %copy-start.3 = (pred[8,16,24,32]{3,2,1,0:T(8,128)(4,1)S(1)}, pred[8,16,24,32]{3,2,1,0:T(8,128)(4,1)}, u32[]{:S(2)}) copy-start(pred[8,16,24,32]{3,2,1,0:T(8,128)(4,1)} %and_or_fusion) | copy-start | bytes 294916
  167.3 15.2 %copy-start.17 = (bf16[8,2,16,48]{3,2,1,0:T(8,128)(2,1)S(1)}, bf16[8,2,16,48]{3,2,1,0:T(8,128)(2,1)}, u32[]{:S(2)}) copy-start(bf16[8,2,16,48]{3,2,1,0:T(8,128)(2,1)} %get-tuple-element.6) | copy-start | bytes 73732
  168.4 72.5 %collective-permute-start.2 = (bf16[24,8,1536]{2,1,0:T(8,128)(2,1)}, bf16[24,8,1536]{2,1,0:T(8,128)(2,1)}, u32[]{:S(2)}, u32[]{:S(2)}) collective-permute-start(bf16[24,8,1536]{2,1,0:T(8,128)(2,1)} %get-tuple-element.28), channel_id=1, source_target_pairs={{0,1},{1,2},{2,3},{3,4},{4,5},{5,6},{6,7},{7,8},{8,9},{9,10},{10,1... | collective-permute-start | bytes 1769480 | tf_op jit(solution)/shard_map/ppermute | solution.py:21
  172.2 68.7 %collective-permute-start.3 = (bf16[24,8,1536]{2,1,0:T(8,128)(2,1)}, bf16[24,8,1536]{2,1,0:T(8,128)(2,1)}, u32[]{:S(2)}, u32[]{:S(2)}) collective-permute-start(bf16[24,8,1536]{2,1,0:T(8,128)(2,1)} %get-tuple-element.29), channel_id=1, source_target_pairs={{1,0},{2,1},{3,2},{4,3},{5,4},{6,5},{7,6},{8,7},{9,8},{10,9},{11,1... | collective-permute-start | bytes 1769480 | tf_op jit(solution)/shard_map/ppermute | solution.py:22
  253.2 5.8 %copy-start.31 = (bf16[128,96]{0,1:T(8,128)(2,1)S(1)}, bf16[128,96]{0,1:T(8,128)(2,1)}, u32[]{:S(2)}) copy-start(bf16[128,96]{0,1:T(8,128)(2,1)} %copy.213) | copy-start | bytes 73732
  254.4 4.9 %copy-start.30 = (bf16[128,96]{0,1:T(8,128)(2,1)S(1)}, bf16[128,96]{0,1:T(8,128)(2,1)}, u32[]{:S(2)}) copy-start(bf16[128,96]{0,1:T(8,128)(2,1)} %copy.215) | copy-start | bytes 73732
  258.9 2.8 copy-start.15
  259.3 3.0 %copy-start.33 = (f32[2,128]{1,0:T(2,128)}, f32[2,128]{1,0:T(2,128)S(1)}, u32[]{:S(2)}) copy-start(f32[2,128]{1,0:T(2,128)S(1)} %get-tuple-element.74) | copy-start | bytes 3076
  259.3 2.7 copy-start.29
  259.6 3.0 %copy-start.34 = (f32[2,128]{1,0:T(2,128)}, f32[2,128]{1,0:T(2,128)S(1)}, u32[]{:S(2)}) copy-start(f32[2,128]{1,0:T(2,128)S(1)} %get-tuple-element.76) | copy-start | bytes 3076
  259.7 2.7 copy-start.28
  264.8 2.3 copy-start.8
  264.8 2.3 copy-start.24
  265.9 4.5 %copy-start.10 = (bf16[768,96]{0,1:T(8,128)(2,1)S(1)}, bf16[768,96]{0,1:T(8,128)(2,1)}, u32[]{:S(2)}) copy-start(bf16[768,96]{0,1:T(8,128)(2,1)} %copy.234) | copy-start | bytes 442372
  266.2 5.8 %copy-start.9 = (bf16[768,96]{0,1:T(8,128)(2,1)S(1)}, bf16[768,96]{0,1:T(8,128)(2,1)}, u32[]{:S(2)}) copy-start(bf16[768,96]{0,1:T(8,128)(2,1)} %copy.235) | copy-start | bytes 442372
  267.1 7.1 %copy-start.32 = (f32[128,16]{0,1:T(8,128)S(1)}, f32[128,16]{0,1:T(8,128)}, u32[]{:S(2)}) copy-start(f32[128,16]{0,1:T(8,128)} %reshape.588) | copy-start | bytes 24580
  268.1 3.9 %copy-start.39 = (f32[2,128]{1,0:T(2,128)S(1)}, f32[2,128]{1,0:T(2,128)}, u32[]{:S(2)}) copy-start(f32[2,128]{1,0:T(2,128)} %get-tuple-element.88) | copy-start | bytes 3076
  268.1 7.3 %copy-start.2 = (f32[128,768]{0,1:T(8,128)S(1)}, f32[128,768]{0,1:T(8,128)}, u32[]{:S(2)}) copy-start(f32[128,768]{0,1:T(8,128)} %copy.202) | copy-start | bytes 1179652
  (13 other events, 21.7 us)
where the time goes:
time: 278 us; the launch traced here: 276 us
  local copies, waits for them, and re-layouts  109 us (39%)
  blocking collectives  108 us (39%)
  other arithmetic  34.9 us (13%)
  matrix products  14.1 us (5%)
  starting transfers between devices  10.2 us (4%)
    gather x1, local copies, waits for them, and re-layouts, dilation_valid_mask(): tissue_keys = tissue[row_indices[:, None], key_columns]  65 us
    all_gather x1, blocking collectives, per_device(): lax.all_gather(key_selected, 'col', axis=1, tiled=True)  55.9 us
    all_gather x1, blocking collectives, per_device(): lax.all_gather(value_selected, 'col', axis=1, tiled=True)  51.7 us
    unnamed x107, local copies, waits for them, and re-layouts  21.9 us
    shift_left x1, other arithmetic, dilation_valid_mask(): jnp.left_shift(jnp.int32(DILATION_MIN), dilation_levels[head_indices])  10 us
    shift_right_arithmetic x1, other arithmetic, dilation_valid_mask(): jnp.right_shift(jnp.int32(column_total), segment_levels[head_indices])  10 us
    ppermute x2, starting transfers between devices, padded_2(): before = lax.ppermute(last, axis, up)  6.23 us
  transfers between devices with their start and end apart: 4, of which 0 were waited for; matrix products, arithmetic and copies ran while one was open for 43% of the time, Pallas kernels for 0%

commit v1 on v0

--- a/solution.py
+++ b/solution.py
@@ -173,9 +173,18 @@
         jnp.where(phase_table, value_phases, zero_entry), axis=2, dtype=jnp.bfloat16
     ).reshape(device_rows, local_selection, model_width)
     token_count = device_rows * HEAD_COUNT
+    tell_scales_for = lambda vector, row_axis: jnp.concatenate(
+        lax.all_to_all(
+            jnp.stack([vector for _ in range(lax.axis_size(row_axis))]),
+            axis_name=row_axis,
+            split_axis=0,
+            concat_axis=0,
+        ),
+        1,
+    )
     k_all, v_all = (
         lax.all_gather(key_selected, "col", axis=1, tiled=True),
-        lax.all_gather(value_selected, "col", axis=1, tiled=True),
+        tell_scales_for(value_selected, "col"),
     )
     key_grid = k_all.reshape(device_rows, selected_count, HEAD_COUNT, head_dimension)
     value_grid = v_all.reshape(device_rows, selected_count, HEAD_COUNT, head_dimension)

time: 278 us -> 261 us (0.939)
  blocking collectives: 108 us -> 60 us
  starting transfers between devices: 10.2 us -> 24.1 us
  matrix products: 14.1 us -> 22.7 us
  local copies, waits for them, and re-layouts: 109 us -> 117 us
    all_gather x1 -> x0, blocking collectives: 51.7 us -> none  [per_device(): lax.all_gather(value_selected, 'col', axis=1, tiled=True)]
    all_to_all x0 -> x1, starting transfers between devices: none -> 13.3 us  [per_device(): lax.all_to_all(jnp.stack([vector for _ in range(lax.axis_size(row_axis))]...]
    unnamed x107 -> x131, local copies, waits for them, and re-layouts: 21.9 us -> 27.7 us
    another operation x0 -> x4, local copies, waits for them, and re-layouts: none -> 5.6 us  [the longest x1 4.52 us: per_device(): v_all.reshape(device_rows, selected_count, HEAD_COUNT, head_dimension)]
    dot_general x8, matrix products: 4.9 us -> 10.2 us  [window_part(): jnp.einsum('hqk,khd->qhd', exp_terms.astype(jnp.bfloat16), value_grp, pre...]
    all_gather x1, blocking collectives: 55.9 us -> 60 us  [per_device(): lax.all_gather(key_selected, 'col', axis=1, tiled=True)]
  transfers between devices with their start and end apart: 4 -> 5, of which waited for: 0 -> 0; matrix products, arithmetic and copies ran while one was open for 43% -> 62% of each run, Pallas kernels for 0% -> 0%
where the time goes in v1:
time: 261 us; the launch traced here: 258 us
  local copies, waits for them, and re-layouts  117 us (45%)
  blocking collectives  60 us (23%)
  other arithmetic  33.5 us (13%)
  starting transfers between devices  24.1 us (9%)
  matrix products  22.7 us (9%)
    gather x1, local copies, waits for them, and re-layouts, dilation_valid_mask(): tissue_keys = tissue[row_indices[:, None], key_columns]  65 us
    all_gather x1, blocking collectives, per_device(): lax.all_gather(key_selected, 'col', axis=1, tiled=True)  60 us
    unnamed x131, local copies, waits for them, and re-layouts  27.7 us
    all_to_all x1, starting transfers between devices, per_device(): lax.all_to_all(jnp.stack([vector for _ in range(lax.axis_size(row_axis))]...  13.3 us
    dot_general x8, matrix products, window_part(): jnp.einsum('hqk,khd->qhd', exp_terms.astype(jnp.bfloat16), value_grp, pre...  10.2 us
    shift_left x1, other arithmetic, dilation_valid_mask(): jnp.left_shift(jnp.int32(DILATION_MIN), dilation_levels[head_indices])  10.1 us
    shift_right_arithmetic x1, other arithmetic, dilation_valid_mask(): jnp.right_shift(jnp.int32(column_total), segment_levels[head_indices])  10.1 us
    ppermute x2, starting transfers between devices, padded_2(): before = lax.ppermute(last, axis, up)  6.86 us
  transfers between devices with their start and end apart: 5, of which 0 were waited for; matrix products, arithmetic and copies ran while one was open for 62% of the time, Pallas kernels for 0%

profile of v1, /device:TPU:56, one launch (start us, length us, event | category | flops | bytes accessed | tf_op | source)
XLA Modules:
  0.0 258.0 jit_solution(6287952241443019224)
XLA Ops:
  2.0 2.7 %collective-permute-start.1 = (bf16[8,16,1536]{2,1,0:T(8,128)(2,1)S(1)}, bf16[8,16,1536]{2,1,0:T(8,128)(2,1)}, u32[]{:S(2)}, u32[]{:S(2)}) collective-permute-start(bf16[8,16,1536]{2,1,0:T(8,128)(2,1)S(1)} %constant_dynamic-update-slice_fusion), channel_id=1, source_target_pairs={{32,0},{64,32},{96,64},{128,96},{160,128},{192,160},{224,192},{256... | collective-permute-start | bytes 1179656 | tf_op jit(solution)/shard_map/ppermute | solution.py:22
  4.7 2.4 collective-permute-start
  7.1 1.6 reshape.569
  8.7 1.6 reshape.583
  12.4 13.3 %all-to-all-start = ((bf16[32,8,2,768]{3,1,2,0:T(8,128)(2,1)}), bf16[32,8,2,768]{3,1,2,0:T(8,128)(2,1)}, u32[]{:S(2)}, u32[]{:S(2)}) async-start(bf16[32,8,2,768]{3,1,2,0:T(8,128)(2,1)} %stack.3), calls=%async_computation | async-start | bytes 1572864 | tf_op jit(solution)/shard_map/all_to_all | solution.py:177
  26.5 10.1 %fusion.103 = s32[128]{0:T(128)S(1)} fusion(s32[]{:T(128)} %bitcast.62, s32[]{:T(128)} %bitcast.63, s32[]{:T(128)} %bitcast.64, s32[]{:T(128)} %bitcast.65, s32[]{:T(128)} %bitcast.66, s32[]{:T(128)} %bitcast.68, s32[]{:T(128)} %bitcast.67, s32[]{:T(128)} %bitcast.53, s32[]{:T(128)} %bitcast.54, s32[]{:T(128)} %bitcast.55, s32[]{:T(128)} %bitcast.56, ...), kind=kLoop, calls=%fused_computation.192 | loop fusion | flops 5120 | bytes 576 | tf_op jit(solution)/shard_map/shift_left | solution.py:94
  37.6 10.1 %fusion.102 = s32[128]{0:T(128)S(1)} fusion(s32[]{:T(128)} %bitcast.45, s32[]{:T(128)} %bitcast.46, s32[]{:T(128)} %bitcast.47, s32[]{:T(128)} %bitcast.48, s32[]{:T(128)} %bitcast.49, s32[]{:T(128)} %bitcast.51, s32[]{:T(128)} %bitcast.50, s32[]{:T(128)} %bitcast.28, s32[]{:T(128)} %bitcast.30, s32[]{:T(128)} %bitcast.32, s32[]{:T(128)} %bitcast.34, ...), kind=kLoop, calls=%fused_computation.191 | loop fusion | flops 5120 | bytes 576 | tf_op jit(solution)/shard_map/shift_right_arithmetic | solution.py:95
  48.0 65.0 %gather_fusion = s32[8192]{0:T(1024)S(1)} fusion(s32[128,512]{1,0:T(8,128)S(1)} %copy-done.1, s32[8192]{0:T(1024)S(1)} %reshape.611), kind=kCustom, calls=%fused_computation | custom fusion | bytes 131072 | tf_op jit(solution)/shard_map/gather | solution.py:93
  119.2 4.5 %collective-permute-start.2 = (bf16[24,8,1536]{2,1,0:T(8,128)(2,1)}, bf16[24,8,1536]{2,1,0:T(8,128)(2,1)}, u32[]{:S(2)}, u32[]{:S(2)}) collective-permute-start(bf16[24,8,1536]{2,1,0:T(8,128)(2,1)} %get-tuple-element.28), channel_id=1, source_target_pairs={{0,1},{1,2},{2,3},{3,4},{4,5},{5,6},{6,7},{7,8},{8,9},{9,10},{10,1... | collective-permute-start | bytes 1769480 | tf_op jit(solution)/shard_map/ppermute | solution.py:21
  123.7 1.3 collective-permute-start.3
  125.0 60.0 %all_gather.3 = bf16[8,64,768]{2,0,1:T(8,128)(2,1)S(1)} all-gather(bf16[8,2,768]{2,0,1:T(8,128)(2,1)S(1)} %copy.181), channel_id=1, replica_groups=mesh['row'=16,'col'=32] {'col'}, dimensions={1}, use_global_device_ids=true | all-gather | bytes 811008 | tf_op jit(solution)/shard_map/all_gather | solution.py:186
  191.2 1.5 broadcast_in_dim.102
  193.0 1.9 copy.182
  194.9 2.0 fusion.118
  199.4 1.7 pad_maximum_fusion
  201.3 1.5 fusion.113
  202.8 1.7 copy.232
  204.5 1.7 copy.231
  206.2 1.7 copy.230
  207.9 1.6 fusion.112
  212.7 1.7 copy.222
  214.4 1.7 copy.220
  229.2 1.6 fusion.45
  231.5 1.7 copy.237
  233.3 1.7 copy.236
  235.0 1.7 copy.235
  238.3 1.9 fusion.27
  240.3 2.1 fusion.26
  242.4 1.8 fusion.25
  245.1 1.8 fusion.23
  247.9 4.5 %reshape_reshape.3 = bf16[8,64,16,48]{3,2,0,1:T(8,128)(2,1)} reshape(bf16[8,32,2,768]{3,0,2,1:T(8,128)(2,1)} %bitcast.92) | data formatting | bytes 1572864 | tf_op jit(solution)/shard_map/reshape;reshape | solution.py:190
  252.5 3.4 %fusion.2 = f32[8,16,16,48]{3,1,2,0:T(8,128)S(1)} fusion(bf16[8,64,16,48]{3,2,0,1:T(8,128)(2,1)} %reshape_reshape.3, f32[8,16,16,64]{3,2,1,0:T(8,128)S(1)} %get-tuple-element.73, f32[8,16,16]{2,1,0:T(8,128)S(1)} %copy-done.13, s32[8,16,16]{2,1,0:T(8,128)S(1)} %copy-done.11, s32[8,16,64]{2,1,0:T(8,128)S(1)} %copy-done.9, pred[8,16,64]{2,1,0:T(8,128)(4,1)S(1)} %copy-done.26), kind=kOutput, calls=%fused_computation.5 | convolution fusion | flops 13238272 | bytes 1761280 | tf_op jit(solution)/shard_map/rhcs,rshw->rchw/dot_general | solution.py:112
  (190 shorter events, 43.5 us)
Async XLA Ops:
  0.0 256.9 %copy-start = (bf16[768,768]{1,0:T(8,128)(2,1)S(1)}, bf16[768,768]{1,0:T(8,128)(2,1)}, u32[]{:S(2)}) copy-start(bf16[768,768]{1,0:T(8,128)(2,1)} %param.16) | copy-start | bytes 3538948
  2.0 114.9 %collective-permute-start.1 = (bf16[8,16,1536]{2,1,0:T(8,128)(2,1)S(1)}, bf16[8,16,1536]{2,1,0:T(8,128)(2,1)}, u32[]{:S(2)}, u32[]{:S(2)}) collective-permute-start(bf16[8,16,1536]{2,1,0:T(8,128)(2,1)S(1)} %constant_dynamic-update-slice_fusion), channel_id=1, source_target_pairs={{32,0},{64,32},{96,64},{128,96},{160,128},{192,160},{224,192},{256... | collective-permute-start | bytes 1179656 | tf_op jit(solution)/shard_map/ppermute | solution.py:22
  4.7 112.2 %collective-permute-start = (bf16[8,16,1536]{2,1,0:T(8,128)(2,1)S(1)}, bf16[8,16,1536]{2,1,0:T(8,128)(2,1)}, u32[]{:S(2)}, u32[]{:S(2)}) collective-permute-start(bf16[8,16,1536]{2,1,0:T(8,128)(2,1)S(1)} %constant_dynamic-update-slice_fusion), channel_id=1, source_target_pairs={{0,32},{32,64},{64,96},{96,128},{128,160},{160,192},{192,224},{224... | collective-permute-start | bytes 1179656 | tf_op jit(solution)/shard_map/ppermute | solution.py:21
  8.7 17.1 %copy-start.27 = (s32[16]{0:T(128)S(1)}, s32[16]{0:T(128)}, u32[]{:S(2)}) copy-start(s32[16]{0:T(128)} %param.14) | copy-start | bytes 196
  8.7 28.2 %copy-start.28 = (s32[16]{0:T(128)S(1)}, s32[16]{0:T(128)}, u32[]{:S(2)}) copy-start(s32[16]{0:T(128)} %param.15) | copy-start | bytes 196
  8.7 39.3 %copy-start.1 = (s32[128,512]{1,0:T(8,128)S(1)}, s32[128,512]{1,0:T(8,128)}, u32[]{:S(2)}) copy-start(s32[128,512]{1,0:T(8,128)} %param.13) | copy-start | bytes 786436
  12.4 235.5 %all-to-all-start = ((bf16[32,8,2,768]{3,1,2,0:T(8,128)(2,1)}), bf16[32,8,2,768]{3,1,2,0:T(8,128)(2,1)}, u32[]{:S(2)}, u32[]{:S(2)}) async-start(bf16[32,8,2,768]{3,1,2,0:T(8,128)(2,1)} %stack.3), calls=%async_computation | async-start | bytes 1572864 | tf_op jit(solution)/shard_map/all_to_all | solution.py:177
  48.0 65.1 %copy-start.7 = (bf16[8,16,768]{2,1,0:T(8,128)(2,1)S(1)}, bf16[8,16,768]{2,1,0:T(8,128)(2,1)}, u32[]{:S(2)}) copy-start(bf16[8,16,768]{2,1,0:T(8,128)(2,1)} %param.10) | copy-start | bytes 589828
  48.0 67.8 %copy-start.23 = (pred[8,16,24,32]{3,2,1,0:T(8,128)(4,1)S(1)}, pred[8,16,24,32]{3,2,1,0:T(8,128)(4,1)}, u32[]{:S(2)}) copy-start(pred[8,16,24,32]{3,2,1,0:T(8,128)(4,1)} %constant.109.clone) | copy-start | bytes 294916
  48.0 67.8 %copy-start.24 = (pred[8,16,24,32]{3,2,1,0:T(8,128)(4,1)S(1)}, pred[8,16,24,32]{3,2,1,0:T(8,128)(4,1)}, u32[]{:S(2)}) copy-start(pred[8,16,24,32]{3,2,1,0:T(8,128)(4,1)} %constant.108.clone) | copy-start | bytes 294916
  114.0 83.6 %copy-start.8 = (s32[8,16,64]{2,1,0:T(8,128)}, s32[8,16,64]{2,1,0:T(8,128)S(1)}, u32[]{:S(2)}) copy-start(s32[8,16,64]{2,1,0:T(8,128)S(1)} %add_select_fusion.1) | copy-start | bytes 98308
  114.8 82.9 %copy-start.10 = (s32[8,16,16]{2,1,0:T(8,128)}, s32[8,16,16]{2,1,0:T(8,128)S(1)}, u32[]{:S(2)}) copy-start(s32[8,16,16]{2,1,0:T(8,128)S(1)} %add_select_fusion) | copy-start | bytes 24580
  115.5 82.1 %copy-start.25 = (pred[8,16,64]{2,1,0:T(8,128)(4,1)}, pred[8,16,64]{2,1,0:T(8,128)(4,1)S(1)}, u32[]{:S(2)}) copy-start(pred[8,16,64]{2,1,0:T(8,128)(4,1)S(1)} %fusion.84) | copy-start | bytes 24580
  119.2 80.2 %collective-permute-start.2 = (bf16[24,8,1536]{2,1,0:T(8,128)(2,1)}, bf16[24,8,1536]{2,1,0:T(8,128)(2,1)}, u32[]{:S(2)}, u32[]{:S(2)}) collective-permute-start(bf16[24,8,1536]{2,1,0:T(8,128)(2,1)} %get-tuple-element.28), channel_id=1, source_target_pairs={{0,1},{1,2},{2,3},{3,4},{4,5},{5,6},{6,7},{7,8},{8,9},{9,10},{10,1... | collective-permute-start | bytes 1769480 | tf_op jit(solution)/shard_map/ppermute | solution.py:21
  123.7 75.7 %collective-permute-start.3 = (bf16[24,8,1536]{2,1,0:T(8,128)(2,1)}, bf16[24,8,1536]{2,1,0:T(8,128)(2,1)}, u32[]{:S(2)}, u32[]{:S(2)}) collective-permute-start(bf16[24,8,1536]{2,1,0:T(8,128)(2,1)} %get-tuple-element.29), channel_id=1, source_target_pairs={{1,0},{2,1},{3,2},{4,3},{5,4},{6,5},{7,6},{8,7},{9,8},{10,9},{11,1... | collective-permute-start | bytes 1769480 | tf_op jit(solution)/shard_map/ppermute | solution.py:22
  209.5 8.8 %copy-start.16 = (bf16[768,96]{1,0:T(8,128)(2,1)S(1)}, bf16[768,96]{1,0:T(8,128)(2,1)}, u32[]{:S(2)}) copy-start(bf16[768,96]{1,0:T(8,128)(2,1)} %get-tuple-element.19) | copy-start | bytes 442372
  218.4 4.3 %copy-start.20 = (bf16[768,96]{0,1:T(8,128)(2,1)S(1)}, bf16[768,96]{0,1:T(8,128)(2,1)}, u32[]{:S(2)}) copy-start(bf16[768,96]{0,1:T(8,128)(2,1)} %copy.231) | copy-start | bytes 442372
  226.9 4.6 %copy-start.35 = (f32[128,16]{0,1:T(8,128)S(1)}, f32[128,16]{0,1:T(8,128)}, u32[]{:S(2)}) copy-start(f32[128,16]{0,1:T(8,128)} %reshape.573) | copy-start | bytes 24580
  226.9 4.6 %copy-start.36 = (f32[128,16]{0,1:T(8,128)S(1)}, f32[128,16]{0,1:T(8,128)}, u32[]{:S(2)}) copy-start(f32[128,16]{0,1:T(8,128)} %reshape.586) | copy-start | bytes 24580
  228.1 8.6 %copy-start.15 = (bf16[768,96]{1,0:T(8,128)(2,1)S(1)}, bf16[768,96]{1,0:T(8,128)(2,1)}, u32[]{:S(2)}) copy-start(bf16[768,96]{1,0:T(8,128)(2,1)} %get-tuple-element.23) | copy-start | bytes 442372
  228.1 9.4 %copy-start.14 = (bf16[768,96]{1,0:T(8,128)(2,1)S(1)}, bf16[768,96]{1,0:T(8,128)(2,1)}, u32[]{:S(2)}) copy-start(bf16[768,96]{1,0:T(8,128)(2,1)} %get-tuple-element.24) | copy-start | bytes 442372
  228.4 11.9 %copy-start.40 = (f32[2,128]{1,0:T(2,128)S(1)}, f32[2,128]{1,0:T(2,128)}, u32[]{:S(2)}) copy-start(f32[2,128]{1,0:T(2,128)} %copy-done.39) | copy-start | bytes 3076
  229.2 13.2 %copy-start.42 = (f32[2,128]{1,0:T(2,128)S(1)}, f32[2,128]{1,0:T(2,128)}, u32[]{:S(2)}) copy-start(f32[2,128]{1,0:T(2,128)} %copy-done.41) | copy-start | bytes 3076
  236.7 8.4 %copy-start.44 = (f32[2,128]{1,0:T(2,128)S(1)}, f32[2,128]{1,0:T(2,128)}, u32[]{:S(2)}) copy-start(f32[2,128]{1,0:T(2,128)} %copy-done.43) | copy-start | bytes 3076
  237.5 6.6 %copy-start.21 = (bf16[768,96]{0,1:T(8,128)(2,1)S(1)}, bf16[768,96]{0,1:T(8,128)(2,1)}, u32[]{:S(2)}) copy-start(bf16[768,96]{0,1:T(8,128)(2,1)} %copy.236) | copy-start | bytes 442372
  238.3 4.1 %copy-start.4 = (f32[2,128,768]{1,2,0:T(8,128)S(1)}, f32[2,128,768]{1,2,0:T(8,128)}, u32[]{:S(2)}) copy-start(f32[2,128,768]{1,2,0:T(8,128)} %copy-done.3) | copy-start | bytes 2359300
  238.3 5.8 %copy-start.5 = (f32[2,128,768]{1,2,0:T(8,128)S(1)}, f32[2,128,768]{1,2,0:T(8,128)}, u32[]{:S(2)}) copy-start(f32[2,128,768]{1,2,0:T(8,128)} %get-tuple-element.87) | copy-start | bytes 2359300
  238.3 6.7 %copy-start.6 = (f32[2,128,768]{1,2,0:T(8,128)S(1)}, f32[2,128,768]{1,2,0:T(8,128)}, u32[]{:S(2)}) copy-start(f32[2,128,768]{1,2,0:T(8,128)} %get-tuple-element.89) | copy-start | bytes 2359300
  245.0 7.4 %copy-start.9 = (s32[8,16,64]{2,1,0:T(8,128)S(1)}, s32[8,16,64]{2,1,0:T(8,128)}, u32[]{:S(2)}) copy-start(s32[8,16,64]{2,1,0:T(8,128)} %copy-done.8) | copy-start | bytes 98308
  245.0 7.4 %copy-start.11 = (s32[8,16,16]{2,1,0:T(8,128)S(1)}, s32[8,16,16]{2,1,0:T(8,128)}, u32[]{:S(2)}) copy-start(s32[8,16,16]{2,1,0:T(8,128)} %copy-done.10) | copy-start | bytes 24580
  245.0 7.4 %copy-start.13 = (f32[8,16,16]{2,1,0:T(8,128)S(1)}, f32[8,16,16]{2,1,0:T(8,128)}, u32[]{:S(2)}) copy-start(f32[8,16,16]{2,1,0:T(8,128)} %copy-done.12) | copy-start | bytes 24580
  245.0 7.4 %copy-start.26 = (pred[8,16,64]{2,1,0:T(8,128)(4,1)S(1)}, pred[8,16,64]{2,1,0:T(8,128)(4,1)}, u32[]{:S(2)}) copy-start(pred[8,16,64]{2,1,0:T(8,128)(4,1)} %copy-done.25) | copy-start | bytes 24580
  (26 other events, 70.2 us)
